TPU v7x, 32 devices: a whole 2x2x4 slice. The times are simulated.
32 devices in a mesh: hour: 16 (over z, y, x), region: 2 (over core).
Axes of the slice: x: 2, y: 2, z: 4, core: 2. Of those that a mesh axis runs over, the one named last changes fastest.
Arguments:
- demand: float32 [2240, 1024], P('hour', 'region'), may hold values from 0.2 to 2
- avail_factor: bfloat16 [2240, 8, 1024], P('hour', None, 'region'), may hold values from 0 to 1
- tech_mask: int32 [8, 1024], P(None, 'region'), may hold values 0 or 1
- var_cost: float32 [8, 1024], P(None, 'region'), may hold values from 0.1 to 2
- inv_cost: float32 [8, 1024], P(None, 'region'), may hold values from 0.2 to 1
- ramp_rate: float32 [8, 1024], P(None, 'region'), may hold values from 0.1 to 1
- network: float32 [1024, 1024], P('region'), as said below
- pattern: int32 [8, 8], replicated, may hold values from 0 to 1, as said below
- live_hours: int32 [1], replicated, may hold values from 1961 to 2100
- generation: float32 [2240, 8, 1024], P('hour', None, 'region'), may hold values from 0 to 1
- angles: float32 [2240, 1024], P('hour', 'region'), may hold values from -3 to 3
- levels: float32 [2240, 1024], P('hour', 'region'), may hold values from 0 to 2
- net_power: float32 [2240, 1024], P('hour', 'region'), may hold values from -3 to 3
- capacity: float32 [8, 1024], P(None, 'region'), may hold values from 0.5 to 2
- balance_dual: float32 [2240, 1024], P('hour', 'region'), may hold values from -3 to 3
- storage_dual: float32 [2240, 1024], P('hour', 'region'), may hold values from -3 to 3
- limit_dual: float32 [2240, 8, 1024], P('hour', None, 'region'), may hold values from 0 to 1.5
- ramp_dual: float32 [2240, 8, 1024], P('hour', None, 'region'), may hold values from 0 to 0.5
Outputs:
- final_generation: float32 [2240, 8, 1024], P('hour', None, 'region')
- final_angles: float32 [2240, 1024], P('hour', 'region')
- final_levels: float32 [2240, 1024], P('hour', 'region')
- final_power: float32 [2240, 1024], P('hour', 'region')
- final_capacity: float32 [8, 1024], P(None, 'region')
- final_balance: float32 [2240, 1024], P('hour', 'region')
- final_storage: float32 [2240, 1024], P('hour', 'region')
- final_limit: float32 [2240, 8, 1024], P('hour', None, 'region')
- final_ramp: float32 [2240, 8, 1024], P('hour', None, 'region')
Inputs may be any that keep to these rules, and one draw needn't show every extreme that they name: pattern is symmetric with ones on its diagonal. network is symmetric.
All inputs are finite; a program needn't handle non-finite values. No bound on the sum of `tech_mask` on one device may be relied on, other than what follows from the above.
Results may differ from a plain program's by a relative error of at most 0.0003.
Values sent between devices are 32-bit elements; how exact they have to be, the bound alone decides.
No kernel may reach another device: no remote copies, remote signals or barrier semaphores. Data moves between devices by JAX's collectives and lax.ppermute only.
A program may use at most 64 MiB of HBM per device.

v0:
```python
import jax
import jax.numpy as jnp
from jax import lax
from jax.sharding import PartitionSpec as P

BUS = 1024
TECH = 8
BLOCK = 128
ITERS = 2
primal_step = 0.2
capacity_step = 4.0
dual_scale = 0.06


def shifted(block, axis, distance):
    devices = range(lax.axis_size(axis))
    route = [((i - distance) % len(devices), i) for i in devices]
    return lax.ppermute(block, axis, route)


def per_device(
    demand,
    avail_factor,
    tech_mask,
    var_cost,
    inv_cost,
    ramp_rate,
    network,
    pattern,
    live_hours,
    generation,
    angles,
    levels,
    net_power,
    capacity,
    balance_dual,
    storage_dual,
    limit_dual,
    ramp_dual,
):
    hour_rows = demand.shape[0]
    local_bus = demand.shape[1]
    total_hours = hour_rows * lax.axis_size("hour")
    first_hour = lax.axis_index("hour") * hour_rows
    live_rows = (first_hour + jnp.arange(hour_rows, dtype=jnp.int32) < live_hours[0]).astype(
        jnp.float32
    )
    available = (
        avail_factor.astype(jnp.float32)
        * tech_mask.astype(jnp.float32)[None]
        * live_rows[:, None, None]
    )
    live_load = demand * live_rows[:, None]
    blocks_here = local_bus // BLOCK
    pattern_rows = lax.dynamic_slice_in_dim(
        pattern, lax.axis_index("region") * blocks_here, blocks_here, 0
    )
    block_mask = jnp.repeat(jnp.repeat(pattern_rows.astype(jnp.float32), BLOCK, 0), BLOCK, 1)
    matrix = network * block_mask
    entry_count = float(total_hours * (TECH + 3) * BUS)

    def fold_part(segment):
        return lax.dot_general(
            segment,
            matrix,
            (((1,), (1,)), ((), ())),
            precision=lax.Precision.HIGHEST,
            preferred_element_type=jnp.float32,
        )

    for iteration in range(ITERS):
        behind = shifted((ramp_dual[-1:], storage_dual[-1:]), "hour", 1)
        prev_ramp = jnp.concatenate([behind[0], ramp_dual[:-1]], axis=0)
        prev_store = jnp.concatenate([behind[1], storage_dual[:-1]], axis=0)
        gen_new = jnp.maximum(
            0.0,
            generation
            - primal_step
            * (var_cost[None] + balance_dual[:, None, :] + limit_dual + prev_ramp - ramp_dual),
        )
        ang_new = angles + primal_step * fold_part(
            lax.all_gather(balance_dual, "region", axis=1, tiled=True)
        )
        pow_new = net_power - primal_step * (balance_dual + storage_dual)
        lev_new = jnp.maximum(0.0, levels - primal_step * (prev_store - storage_dual))
        square_part = (
            jnp.sum((gen_new - generation) ** 2)
            + jnp.sum((ang_new - angles) ** 2)
            + jnp.sum((pow_new - net_power) ** 2)
            + jnp.sum((lev_new - levels) ** 2)
        )
        invest_part = jnp.sum(available * limit_dual + ramp_rate[None] * ramp_dual, axis=0)
        invest = lax.psum(invest_part, "hour")
        squares = lax.psum(square_part, ("hour", "region"))
        cap_new = jnp.maximum(
            0.0, capacity - capacity_step * (inv_cost - invest / float(total_hours))
        )
        step_size = jnp.sqrt(squares / entry_count + 1e-06)
        dual_step = dual_scale / step_size
        gen_bar = 2.0 * gen_new - generation
        ang_bar = 2.0 * ang_new - angles
        pow_bar = 2.0 * pow_new - net_power
        lev_bar = 2.0 * lev_new - levels
        cap_bar = 2.0 * cap_new - capacity
        forward = shifted((gen_bar[:1], lev_bar[:1]), "hour", -1)
        next_gen = jnp.concatenate([gen_bar[1:], forward[0]], axis=0)
        next_level = jnp.concatenate([lev_bar[1:], forward[1]], axis=0)
        balance_dual = balance_dual + dual_step * (
            jnp.sum(gen_bar, axis=1)
            + pow_bar
            - fold_part(lax.all_gather(ang_bar, "region", axis=1, tiled=True))
            - live_load
        )
        storage_dual = storage_dual + dual_step * (next_level - lev_bar + pow_bar)
        limit_dual = jnp.maximum(
            0.0, limit_dual + dual_step * (gen_bar - available * cap_bar[None])
        )
        ramp_dual = jnp.maximum(
            0.0, ramp_dual + dual_step * (next_gen - gen_bar - ramp_rate[None] * cap_bar[None])
        )
        generation, angles, net_power, levels, capacity = (
            gen_new,
            ang_new,
            pow_new,
            lev_new,
            cap_new,
        )
    return (
        generation,
        angles,
        levels,
        net_power,
        capacity,
        balance_dual,
        storage_dual,
        limit_dual,
        ramp_dual,
    )


def solution(mesh):
    return jax.shard_map(
        per_device,
        mesh=mesh,
        in_specs=(
            P("hour", "region"),
            P("hour", None, "region"),
            P(None, "region"),
            P(None, "region"),
            P(None, "region"),
            P(None, "region"),
            P("region", None),
            P(),
            P(),
            P("hour", None, "region"),
            P("hour", "region"),
            P("hour", "region"),
            P("hour", "region"),
            P(None, "region"),
            P("hour", "region"),
            P("hour", "region"),
            P("hour", None, "region"),
            P("hour", None, "region"),
        ),
        out_specs=(
            P("hour", None, "region"),
            P("hour", "region"),
            P("hour", "region"),
            P("hour", "region"),
            P(None, "region"),
            P("hour", "region"),
            P("hour", "region"),
            P("hour", None, "region"),
            P("hour", None, "region"),
        ),
        check_vma=False,
    )
```

profile of v0, /device:TPU:0, one launch (start us, length us, event | category | flops | bytes accessed | tf_op | source)
XLA Modules:
  0.0 319.3 jit_solution(14245832103954252068)
XLA Ops:
  1.4 2.9 collective-permute-start.1
  7.2 2.4 all_gather.12
  12.2 3.7 %multiply_subtract_fusion.7 = (f32[140,512]{1,0:T(8,128)S(1)}, f32[]{:T(128)}, f32[140,512]{1,0:T(8,128)}) fusion(f32[140,512]{1,0:T(8,128)S(1)} %copy-done.28, f32[512,1024]{1,0:T(8,128)S(1)} %bitcast_multiply_fusion, f32[140,1024]{1,0:T(8,128)S(1)} %all_gather.12), kind=kOutput, calls=%fused_computation.61 | convolution fusion | flops 881305600 | bytes 3530756 | tf_op jit(solution)/shard_map/dot_general | solution.py:63
  15.9 2.2 all_gather.13
  18.1 3.0 fusion.39
  22.3 3.0 multiply_subtract_fusion.6
  26.1 4.1 %collective-permute-start.4 = (f32[1,512]{1,0:T(1,128)S(1)}, f32[1,512]{1,0:T(1,128)S(1)}, u32[]{:S(2)}, u32[]{:S(2)}) collective-permute-start(f32[1,512]{1,0:T(1,128)S(1)} %slice.69), channel_id=1, source_target_pairs={{2,0},{4,2},{6,4},{8,6},{10,8},{12,10},{14,12},{16,14},{18,16},{20... | collective-permute-start | bytes 6152 | tf_op jit(solution)/shard_map/ppermute | solution.py:18
  30.2 6.1 %fusion.36 = (f32[140,512]{1,0:T(8,128)}, f32[140,8,512]{2,1,0:T(8,128)}, f32[140,8,512]{2,1,0:T(8,128)S(1)}, f32[8,512]{1,0:T(8,128)S(1)}) fusion(f32[140,8,512]{2,1,0:T(8,128)} %param.27, f32[140,8,512]{2,1,0:T(8,128)S(1)} %copy-done.5, f32[139,8,512]{2,1,0:T(8,128)S(1)} %slice-done, f32[1,8,512]{2,1,0:T(8,128)S(1)} %collective-permute-done, ...), kind=kLoop, calls=%fused_computation.74 | loop fusion | flops 10246144 | bytes 15548976 | tf_op jit(solution)/shard_map/reduce_sum | solution.py:109
  41.9 37.6 %psum.28 = f32[]{:T(128)} all-reduce(f32[]{:T(128)S(6)} %add.149), channel_id=1, replica_groups=mesh['hour'=16,'region'=2] {'hour','region'}, use_global_device_ids=true, to_apply=%region_4.0 | all-reduce | flops 1 | bytes 8 | tf_op jit(solution)/shard_map/psum | solution.py:94
  80.3 3.3 %multiply_reduce_fusion.3 = (f32[]{:T(128)}, f32[140,512]{1,0:T(8,128)}, f32[140,512]{1,0:T(8,128)S(1)}, f32[140,512]{1,0:T(8,128)}) fusion(f32[140,512]{1,0:T(8,128)} %get-tuple-element.42, f32[140,512]{1,0:T(8,128)} %param.33, f32[140,512]{1,0:T(8,128)} %param.30, f32[140,512]{1,0:T(8,128)} %copy-done.20, f32[1,512]{1,0:T(1,128)S(1)} %collective-permute-done.4, ...), kind=kLoop, calls=%fused_computation.56 | loop fusion | flops 1361919 | bytes 3441208 | tf_op jit(solution)/shard_map/reduce_sum | solution.py:89
  84.3 2.3 collective-permute-start.5
  86.6 75.0 %psum.29 = f32[8,512]{1,0:T(8,128)S(1)} all-reduce(f32[8,512]{1,0:T(8,128)S(1)} %get-tuple-element.32), channel_id=1, replica_groups=mesh['hour'=16,'region'=2] {'hour'}, use_global_device_ids=true, to_apply=%region_7.0 | all-reduce | flops 4096 | bytes 32768 | tf_op jit(solution)/shard_map/psum | solution.py:93
  162.4 2.6 all_gather.14
  165.0 4.8 %multiply_reduce_fusion.4 = (f32[]{:T(128)}, f32[140,512]{1,0:T(8,128)}, f32[140,512]{1,0:T(8,128)}) fusion(f32[140,512]{1,0:T(8,128)} %get-tuple-element.43, f32[140,1024]{1,0:T(8,128)S(1)} %all_gather.14, f32[512,1024]{1,0:T(8,128)S(1)} %bitcast_multiply_fusion), kind=kOutput, calls=%fused_computation.57 | convolution fusion | flops 881305600 | bytes 3530756 | tf_op jit(solution)/shard_map/dot_general | solution.py:63
  172.6 2.1 collective-permute-start.3
  175.5 4.4 %collective-permute-done.3 = f32[1,8,512]{2,1,0:T(8,128)S(1)} collective-permute-done((f32[1,8,512]{2,1,0:T(8,128)S(1)}, f32[1,8,512]{2,1,0:T(8,128)S(1)}, u32[]{:S(2)}, u32[]{:S(2)}) %collective-permute-start.3) | collective-permute-done | bytes 16416 | tf_op jit(solution)/shard_map/ppermute | solution.py:18
  180.0 4.3 %multiply_reduce_fusion = (f32[]{:T(128)}, f32[140,8,512]{2,1,0:T(8,128)}, f32[140,8,512]{2,1,0:T(8,128)}) fusion(f32[140,8,512]{2,1,0:T(8,128)S(1)} %copy-done.3, f32[140,8,512]{2,1,0:T(8,128)S(1)} %fusion.7, f32[139,8,512]{2,1,0:T(8,128)S(1)} %slice.67, f32[1,8,512]{2,1,0:T(8,128)S(1)} %collective-permute-done.3, f32[140,512]{1,0:T(8,128)S(1)} %copy-done.16, ...), kind=kLoop, calls=%fused_computation.22 | loop fusion | flops 10895359 | bytes 17539640 | tf_op jit(solution)/shard_map/reduce_sum | solution.py:87
  186.8 3.9 %all_gather.15 = f32[140,1024]{1,0:T(8,128)} all-gather(f32[140,512]{1,0:T(8,128)} %get-tuple-element.38), channel_id=1, replica_groups=mesh['hour'=16,'region'=2] {'region'}, dimensions={1}, use_global_device_ids=true | all-gather | bytes 860160 | tf_op jit(solution)/shard_map/all_gather | solution.py:111
  190.7 36.8 %psum.31 = f32[]{:T(128)} all-reduce(f32[]{:T(128)S(6)} %add.169), channel_id=1, replica_groups=mesh['hour'=16,'region'=2] {'hour','region'}, use_global_device_ids=true, to_apply=%region_14.0 | all-reduce | flops 1 | bytes 8 | tf_op jit(solution)/shard_map/psum | solution.py:94
  228.2 2.2 add_reduce_fusion
  230.4 75.8 %psum.30 = f32[8,512]{1,0:T(8,128)S(1)} all-reduce(f32[8,512]{1,0:T(8,128)S(1)} %add_reduce_fusion), channel_id=1, replica_groups=mesh['hour'=16,'region'=2] {'hour'}, use_global_device_ids=true, to_apply=%region_9.0 | all-reduce | flops 4096 | bytes 32768 | tf_op jit(solution)/shard_map/psum | solution.py:93
  306.9 5.3 %add_maximum_fusion = (f32[140,8,512]{2,1,0:T(8,128)}, f32[140,8,512]{2,1,0:T(8,128)S(1)}) fusion(f32[140,8,512]{2,1,0:T(8,128)} %get-tuple-element.22, bf16[140,8,512]{2,1,0:T(8,128)(2,1)S(1)} %copy-done.7, f32[8,512]{1,0:T(8,128)S(1)} %get-tuple-element.10, f32[]{:T(128)S(6)} %div.23, f32[140]{0:T(256)} %copy-done.33, ...), kind=kLoop, calls=%fused_computation.20 | loop fusion | flops 5734400 | bytes 12649012 | tf_op jit(solution)/shard_map/max | solution.py:115
  312.2 2.3 fusion.40
  316.0 2.3 fusion.15
  (114 shorter events, 18.6 us)
Async XLA Ops:
  1.4 20.5 %collective-permute-start.1 = (f32[1,512]{1,0:T(1,128)S(1)}, f32[1,512]{1,0:T(1,128)S(1)}, u32[]{:S(2)}, u32[]{:S(2)}) collective-permute-start(f32[1,512]{1,0:T(1,128)S(1)} %slice.50), channel_id=1, source_target_pairs={{30,0},{0,2},{2,4},{4,6},{6,8},{8,10},{10,12},{12,14},{14,16},{16,... | collective-permute-start | bytes 6152 | tf_op jit(solution)/shard_map/ppermute | solution.py:18
  5.0 25.2 %collective-permute-start = (f32[1,8,512]{2,1,0:T(8,128)S(1)}, f32[1,8,512]{2,1,0:T(8,128)S(1)}, u32[]{:S(2)}, u32[]{:S(2)}) collective-permute-start(f32[1,8,512]{2,1,0:T(8,128)S(1)} %slice.48), channel_id=1, source_target_pairs={{30,0},{0,2},{2,4},{4,6},{6,8},{8,10},{10,12},{12,14},{14,16},{16,... | collective-permute-start | bytes 49160 | tf_op jit(solution)/shard_map/ppermute | solution.py:18
  12.2 152.8 %copy-start = (f32[512,1024]{1,0:T(8,128)}, f32[512,1024]{1,0:T(8,128)S(1)}, u32[]{:S(2)}) copy-start(f32[512,1024]{1,0:T(8,128)S(1)} %bitcast_multiply_fusion) | copy-start | bytes 6291460
  21.1 59.1 %copy-start.33 = (f32[140]{0:T(256)}, f32[140]{0:T(256)S(1)}, u32[]{:S(2)}) copy-start(f32[140]{0:T(256)S(1)} %compare_convert_fusion) | copy-start | bytes 1684
  21.2 9.0 %copy-start.5 = (f32[140,8,512]{2,1,0:T(8,128)S(1)}, f32[140,8,512]{2,1,0:T(8,128)}, u32[]{:S(2)}) copy-start(f32[140,8,512]{2,1,0:T(8,128)} %param.35) | copy-start | bytes 6881284
  21.2 9.0 %copy-start.7 = (bf16[140,8,512]{2,1,0:T(8,128)(2,1)S(1)}, bf16[140,8,512]{2,1,0:T(8,128)(2,1)}, u32[]{:S(2)}) copy-start(bf16[140,8,512]{2,1,0:T(8,128)(2,1)} %param.19) | copy-start | bytes 3440644
  21.9 8.4 %slice-start = ((f32[140,8,512]{2,1,0:T(8,128)}), f32[139,8,512]{2,1,0:T(8,128)S(1)}, s32[]{:S(2)}) async-start(f32[140,8,512]{2,1,0:T(8,128)} %param.35), calls=%async_computation | async-start | bytes 4554752 | tf_op jit(solution)/shard_map/slice | solution.py:73
  21.9 8.4 %copy-start.29 = (f32[8,512]{1,0:T(8,128)S(1)}, f32[8,512]{1,0:T(8,128)}, u32[]{:S(2)}) copy-start(f32[8,512]{1,0:T(8,128)} %param.23) | copy-start | bytes 49156
  21.9 8.4 %copy-start.32 = (f32[8,512]{1,0:T(8,128)S(1)}, f32[8,512]{1,0:T(8,128)}, u32[]{:S(2)}) copy-start(f32[8,512]{1,0:T(8,128)} %param.21) | copy-start | bytes 49156
  25.3 4.8 %copy-start.13 = (f32[140,512]{1,0:T(8,128)}, f32[140,512]{1,0:T(8,128)S(1)}, u32[]{:S(2)}) copy-start(f32[140,512]{1,0:T(8,128)S(1)} %get-tuple-element.24) | copy-start | bytes 860164
  26.1 10.3 %copy-start.8 = (f32[140,8,512]{2,1,0:T(8,128)S(1)}, f32[140,8,512]{2,1,0:T(8,128)}, u32[]{:S(2)}) copy-start(f32[140,8,512]{2,1,0:T(8,128)} %param.27) | copy-start | bytes 6881284
  26.1 54.2 %collective-permute-start.4 = (f32[1,512]{1,0:T(1,128)S(1)}, f32[1,512]{1,0:T(1,128)S(1)}, u32[]{:S(2)}, u32[]{:S(2)}) collective-permute-start(f32[1,512]{1,0:T(1,128)S(1)} %slice.69), channel_id=1, source_target_pairs={{2,0},{4,2},{6,4},{8,6},{10,8},{12,10},{14,12},{16,14},{18,16},{20... | collective-permute-start | bytes 6152 | tf_op jit(solution)/shard_map/ppermute | solution.py:18
  83.6 86.2 %copy-start.30 = (f32[8,512]{1,0:T(8,128)S(1)}, f32[8,512]{1,0:T(8,128)}, u32[]{:S(2)}) copy-start(f32[8,512]{1,0:T(8,128)} %param.31) | copy-start | bytes 49156
  83.6 86.2 %copy-start.31 = (f32[8,512]{1,0:T(8,128)S(1)}, f32[8,512]{1,0:T(8,128)}, u32[]{:S(2)}) copy-start(f32[8,512]{1,0:T(8,128)} %param.22) | copy-start | bytes 49156
  84.3 85.8 %collective-permute-start.5 = (f32[1,512]{1,0:T(1,128)S(1)}, f32[1,512]{1,0:T(1,128)S(1)}, u32[]{:S(2)}, u32[]{:S(2)}) collective-permute-start(f32[1,512]{1,0:T(1,128)S(1)} %slice.70), channel_id=1, source_target_pairs={{30,0},{0,2},{2,4},{4,6},{6,8},{8,10},{10,12},{12,14},{14,16},{16,... | collective-permute-start | bytes 6152 | tf_op jit(solution)/shard_map/ppermute | solution.py:18
  161.5 8.3 %copy-start.4 = (f32[140,8,512]{2,1,0:T(8,128)S(1)}, f32[140,8,512]{2,1,0:T(8,128)}, u32[]{:S(2)}) copy-start(f32[140,8,512]{2,1,0:T(8,128)} %get-tuple-element.26) | copy-start | bytes 6881284
  162.4 9.3 %collective-permute-start.2 = (f32[1,8,512]{2,1,0:T(8,128)S(1)}, f32[1,8,512]{2,1,0:T(8,128)S(1)}, u32[]{:S(2)}, u32[]{:S(2)}) collective-permute-start(f32[1,8,512]{2,1,0:T(8,128)S(1)} %slice.65), channel_id=1, source_target_pairs={{2,0},{4,2},{6,4},{8,6},{10,8},{12,10},{14,12},{16,14},{18,16},{20... | collective-permute-start | bytes 49160 | tf_op jit(solution)/shard_map/ppermute | solution.py:18
  172.6 7.4 %collective-permute-start.3 = (f32[1,8,512]{2,1,0:T(8,128)S(1)}, f32[1,8,512]{2,1,0:T(8,128)S(1)}, u32[]{:S(2)}, u32[]{:S(2)}) collective-permute-start(f32[1,8,512]{2,1,0:T(8,128)S(1)} %slice.66), channel_id=1, source_target_pairs={{30,0},{0,2},{2,4},{4,6},{6,8},{8,10},{10,12},{12,14},{14,16},{16,... | collective-permute-start | bytes 49160 | tf_op jit(solution)/shard_map/ppermute | solution.py:18
  174.7 5.3 %copy-start.9 = (f32[140,8,512]{2,1,0:T(8,128)S(1)}, f32[140,8,512]{2,1,0:T(8,128)}, u32[]{:S(2)}) copy-start(f32[140,8,512]{2,1,0:T(8,128)} %param.34) | copy-start | bytes 6881284
  175.3 4.7 %copy-start.34 = (f32[140]{0:T(256)S(1)}, f32[140]{0:T(256)}, u32[]{:S(2)}) copy-start(f32[140]{0:T(256)} %copy-done.33) | copy-start | bytes 1684
  306.9 5.4 %copy-start.1 = (f32[512,1024]{1,0:T(8,128)S(1)}, f32[512,1024]{1,0:T(8,128)}, u32[]{:S(2)}) copy-start(f32[512,1024]{1,0:T(8,128)} %copy-done) | copy-start | bytes 6291460
  306.9 5.4 %copy-start.22 = (f32[140,1024]{1,0:T(8,128)S(1)}, f32[140,1024]{1,0:T(8,128)}, u32[]{:S(2)}) copy-start(f32[140,1024]{1,0:T(8,128)} %all_gather.15) | copy-start | bytes 1720324
  312.2 3.7 %collective-permute-start.7 = (f32[1,8,512]{2,1,0:T(8,128)S(1)}, f32[1,8,512]{2,1,0:T(8,128)S(1)}, u32[]{:S(2)}, u32[]{:S(2)}) collective-permute-start(f32[1,8,512]{2,1,0:T(8,128)S(1)} %slice.75), channel_id=1, source_target_pairs={{2,0},{4,2},{6,4},{8,6},{10,8},{12,10},{14,12},{16,14},{18,16},{20... | collective-permute-start | bytes 49160 | tf_op jit(solution)/shard_map/ppermute | solution.py:18
  314.6 3.6 %collective-permute-start.6 = (f32[1,512]{1,0:T(1,128)S(1)}, f32[1,512]{1,0:T(1,128)S(1)}, u32[]{:S(2)}, u32[]{:S(2)}) collective-permute-start(f32[1,512]{1,0:T(1,128)S(1)} %slice.73), channel_id=1, source_target_pairs={{2,0},{4,2},{6,4},{8,6},{10,8},{12,10},{14,12},{16,14},{18,16},{20... | collective-permute-start | bytes 6152 | tf_op jit(solution)/shard_map/ppermute | solution.py:18
  (22 other events, 41.7 us)
where the time goes:
time: 320 us; the launch traced here: 319 us
  blocking collectives  236 us (74%)
  other arithmetic  34 us (11%)
  matrix products  13.8 us (4%)
  starting transfers between devices  13 us (4%)
  local copies, waits for them, and re-layouts  8.49 us (3%)
  between operations  8.08 us (3%)
  waiting for transfers between devices  5.53 us (2%)
    psum x2, blocking collectives, per_device(): invest = lax.psum(invest_part, 'hour')  151 us
    psum x2, blocking collectives, per_device(): squares = lax.psum(square_part, ('hour', 'region'))  74.5 us
    dot_general x4, matrix products, fold_part(): lax.dot_general(segment, matrix, (((1,), (1,)), ((), ())), precision=lax....  13.8 us
    ppermute x8, starting transfers between devices, shifted(): return lax.ppermute(block, axis, route)  13 us
  transfers between devices with their start and end apart: 8, of which 2 were waited for; matrix products, arithmetic and copies ran while one was open for 11% of the time, Pallas kernels for 0%

commit v1 on v0

--- a/solution.py
+++ b/solution.py
@@ -90,7 +90,8 @@
             + jnp.sum((lev_new - levels) ** 2)
         )
         invest_part = jnp.sum(available * limit_dual + ramp_rate[None] * ramp_dual, axis=0)
-        invest = lax.psum(invest_part, "hour")
+        blocks = lax.all_gather(invest_part, "hour")
+        invest = jnp.sum(blocks, axis=0)
         squares = lax.psum(square_part, ("hour", "region"))
         cap_new = jnp.maximum(
             0.0, capacity - capacity_step * (inv_cost - invest / float(total_hours))

time: 320 us -> 248 us (0.78)
  blocking collectives: 236 us -> 164 us
    psum x2 -> x0, blocking collectives: 151 us -> none  [per_device(): invest = lax.psum(invest_part, 'hour')]
    all_gather x0 -> x2, blocking collectives: none -> 78.5 us  [per_device(): blocks = lax.all_gather(invest_part, 'hour')]
  transfers between devices with their start and end apart: 8 -> 8, of which waited for: 2 -> 2; matrix products, arithmetic and copies ran while one was open for 11% -> 13% of each run, Pallas kernels for 0% -> 0%
where the time goes in v1:
time: 248 us; the launch traced here: 247 us
  blocking collectives  164 us (66%)
  other arithmetic  33 us (13%)
  starting transfers between devices  15.6 us (6%)
  matrix products  12.9 us (5%)
  between operations  8.24 us (3%)
  local copies, waits for them, and re-layouts  6.81 us (3%)
  waiting for transfers between devices  6.24 us (3%)
    all_gather x2, blocking collectives, per_device(): blocks = lax.all_gather(invest_part, 'hour')  78.5 us
    psum x2, blocking collectives, per_device(): squares = lax.psum(square_part, ('hour', 'region'))  74.5 us
    ppermute x8, starting transfers between devices, shifted(): return lax.ppermute(block, axis, route)  15.6 us
    dot_general x4, matrix products, fold_part(): lax.dot_general(segment, matrix, (((1,), (1,)), ((), ())), precision=lax....  12.9 us
    ppermute x8, waiting for transfers between devices, shifted(): return lax.ppermute(block, axis, route)  6.24 us
    all_gather x2, blocking collectives, per_device(): lax.all_gather(ang_bar, 'region', axis=1, tiled=True)  6.09 us
    reduce_sum x1, other arithmetic, per_device(): jnp.sum(gen_bar, axis=1) + pow_bar  6.08 us
    reduce_sum x2, other arithmetic, per_device(): jnp.sum((gen_new - generation) ** 2) + jnp.sum((ang_new - angles) ** 2)  5.5 us
  transfers between devices with their start and end apart: 8, of which 2 were waited for; matrix products, arithmetic and copies ran while one was open for 13% of the time, Pallas kernels for 0%

profile of v1, /device:TPU:0, one launch (start us, length us, event | category | flops | bytes accessed | tf_op | source)
XLA Modules:
  0.0 246.7 jit_solution(11726881796149759888)
XLA Ops:
  1.4 2.9 %collective-permute-start.1 = (f32[1,512]{1,0:T(1,128)S(1)}, f32[1,512]{1,0:T(1,128)S(1)}, u32[]{:S(2)}, u32[]{:S(2)}) collective-permute-start(f32[1,512]{1,0:T(1,128)S(1)} %slice.50), channel_id=1, source_target_pairs={{30,0},{0,2},{2,4},{4,6},{6,8},{8,10},{10,12},{12,14},{14,16},{16,... | collective-permute-start | bytes 6152 | tf_op jit(solution)/shard_map/ppermute | solution.py:18
  7.2 2.4 all_gather.24
  12.2 3.7 %multiply_subtract_fusion.7 = (f32[140,512]{1,0:T(8,128)S(1)}, f32[]{:T(128)}, f32[140,512]{1,0:T(8,128)}) fusion(f32[140,512]{1,0:T(8,128)S(1)} %copy-done.30, f32[512,1024]{1,0:T(8,128)S(1)} %bitcast_multiply_fusion, f32[140,1024]{1,0:T(8,128)S(1)} %all_gather.24), kind=kOutput, calls=%fused_computation.61 | convolution fusion | flops 881305600 | bytes 3530756 | tf_op jit(solution)/shard_map/dot_general | solution.py:63
  15.9 2.2 all_gather.25
  18.1 3.0 %fusion.39 = f32[140,512]{1,0:T(8,128)} fusion(f32[140,1024]{1,0:T(8,128)S(1)} %all_gather.25, f32[512,1024]{1,0:T(8,128)S(1)} %bitcast_multiply_fusion), kind=kOutput, calls=%fused_computation.78 | convolution fusion | flops 880803840 | bytes 2957312 | tf_op jit(solution)/shard_map/dot_general | solution.py:63
  22.3 3.1 %multiply_subtract_fusion.6 = (f32[140,512]{1,0:T(8,128)S(1)}, f32[140,512]{1,0:T(8,128)S(1)}, f32[]{:T(128)}, f32[140,512]{1,0:T(8,128)}) fusion(f32[140,512]{1,0:T(8,128)S(1)} %copy-done.25, f32[140,512]{1,0:T(8,128)S(1)} %copy-done.19, f32[139,512]{1,0:T(8,128)S(1)} %bitcast.26, f32[1,512]{1,0:T(1,128)S(1)} %collective-permute-done.1, ...), kind=kLoop, calls=%fused_computation.59 | loop fusion | flops 931839 | bytes 2293764 | tf_op jit(solution)/shard_map/sub | solution.py:104
  26.1 4.1 %collective-permute-start.4 = (f32[1,512]{1,0:T(1,128)S(1)}, f32[1,512]{1,0:T(1,128)S(1)}, u32[]{:S(2)}, u32[]{:S(2)}) collective-permute-start(f32[1,512]{1,0:T(1,128)S(1)} %slice.69), channel_id=1, source_target_pairs={{2,0},{4,2},{6,4},{8,6},{10,8},{12,10},{14,12},{16,14},{18,16},{20... | collective-permute-start | bytes 6152 | tf_op jit(solution)/shard_map/ppermute | solution.py:18
  30.3 6.1 %fusion.36 = (f32[140,512]{1,0:T(8,128)}, f32[140,8,512]{2,1,0:T(8,128)}, f32[140,8,512]{2,1,0:T(8,128)S(1)}, f32[8,512]{1,0:T(8,128)S(1)}) fusion(f32[140,8,512]{2,1,0:T(8,128)} %param.27, f32[140,8,512]{2,1,0:T(8,128)S(1)} %copy-done.6, f32[139,8,512]{2,1,0:T(8,128)S(1)} %slice-done, f32[1,8,512]{2,1,0:T(8,128)S(1)} %collective-permute-done, ...), kind=kLoop, calls=%fused_computation.76 | loop fusion | flops 10246144 | bytes 15548976 | tf_op jit(solution)/shard_map/reduce_sum | solution.py:110
  42.1 37.6 %psum.14 = f32[]{:T(128)} all-reduce(f32[]{:T(128)S(6)} %add.145), channel_id=1, replica_groups=mesh['hour'=16,'region'=2] {'hour','region'}, use_global_device_ids=true, to_apply=%region_4.0 | all-reduce | flops 1 | bytes 8 | tf_op jit(solution)/shard_map/psum | solution.py:95
  80.5 3.3 %multiply_reduce_fusion.3 = (f32[]{:T(128)}, f32[140,512]{1,0:T(8,128)}, f32[140,512]{1,0:T(8,128)S(1)}, f32[140,512]{1,0:T(8,128)S(1)}) fusion(f32[140,512]{1,0:T(8,128)} %get-tuple-element.42, f32[140,512]{1,0:T(8,128)} %param.33, f32[140,512]{1,0:T(8,128)} %param.30, f32[140,512]{1,0:T(8,128)} %copy-done.21, f32[1,512]{1,0:T(1,128)S(1)} %collective-permute-done.4, ...), kind=kLoop, calls=%fused_computation.56 | loop fusion | flops 1361919 | bytes 3441208 | tf_op jit(solution)/shard_map/reduce_sum | solution.py:89
  83.8 2.3 collective-permute-start.5
  86.2 3.3 %collective-permute-start.2 = (f32[1,8,512]{2,1,0:T(8,128)S(1)}, f32[1,8,512]{2,1,0:T(8,128)S(1)}, u32[]{:S(2)}, u32[]{:S(2)}) collective-permute-start(f32[1,8,512]{2,1,0:T(8,128)S(1)} %slice.65), channel_id=1, source_target_pairs={{2,0},{4,2},{6,4},{8,6},{10,8},{12,10},{14,12},{16,14},{18,16},{20... | collective-permute-start | bytes 49160 | tf_op jit(solution)/shard_map/ppermute | solution.py:18
  89.5 37.6 %all-gather = f32[128,512]{1,0:T(8,128)S(1)} all-gather(f32[8,512]{1,0:T(8,128)S(1)} %get-tuple-element.32), channel_id=2, replica_groups=mesh['hour'=16,'region'=2] {'hour'}, dimensions={0}, use_global_device_ids=true | all-gather | bytes 278528 | tf_op jit(solution)/shard_map/all_gather | solution.py:93
  127.2 2.4 all_gather.28
  129.6 3.8 %multiply_reduce_fusion.4 = (f32[]{:T(128)}, f32[140,512]{1,0:T(8,128)}, f32[140,512]{1,0:T(8,128)}) fusion(f32[140,512]{1,0:T(8,128)S(1)} %copy-done.29, f32[140,1024]{1,0:T(8,128)S(1)} %all_gather.28, f32[512,1024]{1,0:T(8,128)S(1)} %bitcast_multiply_fusion), kind=kOutput, calls=%fused_computation.57 | convolution fusion | flops 881305600 | bytes 3530756 | tf_op jit(solution)/shard_map/dot_general | solution.py:63
  138.4 5.2 %collective-permute-done.3 = f32[1,8,512]{2,1,0:T(8,128)S(1)} collective-permute-done((f32[1,8,512]{2,1,0:T(8,128)S(1)}, f32[1,8,512]{2,1,0:T(8,128)S(1)}, u32[]{:S(2)}, u32[]{:S(2)}) %collective-permute-start.3) | collective-permute-done | bytes 16416 | tf_op jit(solution)/shard_map/ppermute | solution.py:18
  143.5 4.2 %multiply_reduce_fusion = (f32[]{:T(128)}, f32[140,8,512]{2,1,0:T(8,128)}, f32[140,8,512]{2,1,0:T(8,128)}) fusion(f32[140,8,512]{2,1,0:T(8,128)S(1)} %copy-done.3, f32[140,8,512]{2,1,0:T(8,128)S(1)} %fusion.7, f32[139,8,512]{2,1,0:T(8,128)S(1)} %slice.67, f32[1,8,512]{2,1,0:T(8,128)S(1)} %collective-permute-done.3, f32[140,512]{1,0:T(8,128)S(1)} %get-tuple-element.19, ...), kind=kLoop, calls=%fused_computation.22 | loop fusion | flops 10895359 | bytes 17539640 | tf_op jit(solution)/shard_map/reduce_sum | solution.py:87
  150.3 3.9 %all_gather.31 = f32[140,1024]{1,0:T(8,128)} all-gather(f32[140,512]{1,0:T(8,128)} %get-tuple-element.38), channel_id=1, replica_groups=mesh['hour'=16,'region'=2] {'region'}, dimensions={1}, use_global_device_ids=true | all-gather | bytes 860160 | tf_op jit(solution)/shard_map/all_gather | solution.py:112
  154.1 36.8 %psum.15 = f32[]{:T(128)} all-reduce(f32[]{:T(128)S(6)} %add.165), channel_id=1, replica_groups=mesh['hour'=16,'region'=2] {'hour','region'}, use_global_device_ids=true, to_apply=%region_14.0 | all-reduce | flops 1 | bytes 8 | tf_op jit(solution)/shard_map/psum | solution.py:95
  191.7 2.3 add_reduce_fusion
  194.0 40.9 %all-gather.1 = f32[128,512]{1,0:T(8,128)S(1)} all-gather(f32[8,512]{1,0:T(8,128)S(1)} %add_reduce_fusion), channel_id=3, replica_groups=mesh['hour'=16,'region'=2] {'hour'}, dimensions={0}, use_global_device_ids=true | all-gather | bytes 278528 | tf_op jit(solution)/shard_map/all_gather | solution.py:93
  235.6 4.0 %add_maximum_fusion = (f32[140,8,512]{2,1,0:T(8,128)}, f32[140,8,512]{2,1,0:T(8,128)S(1)}) fusion(f32[140,8,512]{2,1,0:T(8,128)S(1)} %copy-done.8, bf16[140,8,512]{2,1,0:T(8,128)(2,1)S(1)} %copy-done.9, f32[8,512]{1,0:T(8,128)S(1)} %get-tuple-element.10, f32[]{:T(128)S(6)} %div.23, f32[140]{0:T(256)S(1)} %compare_convert_fusion, ...), kind=kLoop, calls=%fused_computation.20 | loop fusion | flops 5734400 | bytes 12649012 | tf_op jit(solution)/shard_map/max | solution.py:116
  239.7 2.3 fusion.40
  243.4 2.3 fusion.15
  (114 shorter events, 18.4 us)
Async XLA Ops:
  1.4 20.5 %collective-permute-start.1 = (f32[1,512]{1,0:T(1,128)S(1)}, f32[1,512]{1,0:T(1,128)S(1)}, u32[]{:S(2)}, u32[]{:S(2)}) collective-permute-start(f32[1,512]{1,0:T(1,128)S(1)} %slice.50), channel_id=1, source_target_pairs={{30,0},{0,2},{2,4},{4,6},{6,8},{8,10},{10,12},{12,14},{14,16},{16,... | collective-permute-start | bytes 6152 | tf_op jit(solution)/shard_map/ppermute | solution.py:18
  5.0 25.2 %collective-permute-start = (f32[1,8,512]{2,1,0:T(8,128)S(1)}, f32[1,8,512]{2,1,0:T(8,128)S(1)}, u32[]{:S(2)}, u32[]{:S(2)}) collective-permute-start(f32[1,8,512]{2,1,0:T(8,128)S(1)} %slice.48), channel_id=1, source_target_pairs={{30,0},{0,2},{2,4},{4,6},{6,8},{8,10},{10,12},{12,14},{14,16},{16,... | collective-permute-start | bytes 49160 | tf_op jit(solution)/shard_map/ppermute | solution.py:18
  12.2 117.4 %copy-start = (f32[512,1024]{1,0:T(8,128)}, f32[512,1024]{1,0:T(8,128)S(1)}, u32[]{:S(2)}) copy-start(f32[512,1024]{1,0:T(8,128)S(1)} %bitcast_multiply_fusion) | copy-start | bytes 6291460
  21.2 9.1 %copy-start.6 = (f32[140,8,512]{2,1,0:T(8,128)S(1)}, f32[140,8,512]{2,1,0:T(8,128)}, u32[]{:S(2)}) copy-start(f32[140,8,512]{2,1,0:T(8,128)} %param.35) | copy-start | bytes 6881284
  21.2 9.1 %copy-start.9 = (bf16[140,8,512]{2,1,0:T(8,128)(2,1)S(1)}, bf16[140,8,512]{2,1,0:T(8,128)(2,1)}, u32[]{:S(2)}) copy-start(bf16[140,8,512]{2,1,0:T(8,128)(2,1)} %param.19) | copy-start | bytes 3440644
  21.8 8.4 %slice-start = ((f32[140,8,512]{2,1,0:T(8,128)}), f32[139,8,512]{2,1,0:T(8,128)S(1)}, s32[]{:S(2)}) async-start(f32[140,8,512]{2,1,0:T(8,128)} %param.35), calls=%async_computation | async-start | bytes 4554752 | tf_op jit(solution)/shard_map/slice | solution.py:73
  21.9 8.4 %copy-start.31 = (f32[8,512]{1,0:T(8,128)S(1)}, f32[8,512]{1,0:T(8,128)}, u32[]{:S(2)}) copy-start(f32[8,512]{1,0:T(8,128)} %param.23) | copy-start | bytes 49156
  21.9 8.4 %copy-start.34 = (f32[8,512]{1,0:T(8,128)S(1)}, f32[8,512]{1,0:T(8,128)}, u32[]{:S(2)}) copy-start(f32[8,512]{1,0:T(8,128)} %param.21) | copy-start | bytes 49156
  26.1 10.3 %copy-start.10 = (f32[140,8,512]{2,1,0:T(8,128)S(1)}, f32[140,8,512]{2,1,0:T(8,128)}, u32[]{:S(2)}) copy-start(f32[140,8,512]{2,1,0:T(8,128)} %param.27) | copy-start | bytes 6881284
  26.1 54.3 %collective-permute-start.4 = (f32[1,512]{1,0:T(1,128)S(1)}, f32[1,512]{1,0:T(1,128)S(1)}, u32[]{:S(2)}, u32[]{:S(2)}) collective-permute-start(f32[1,512]{1,0:T(1,128)S(1)} %slice.69), channel_id=1, source_target_pairs={{2,0},{4,2},{6,4},{8,6},{10,8},{12,10},{14,12},{16,14},{18,16},{20... | collective-permute-start | bytes 6152 | tf_op jit(solution)/shard_map/ppermute | solution.py:18
  80.4 5.7 %copy-start.5 = (f32[140,8,512]{2,1,0:T(8,128)S(1)}, f32[140,8,512]{2,1,0:T(8,128)}, u32[]{:S(2)}) copy-start(f32[140,8,512]{2,1,0:T(8,128)} %get-tuple-element.26) | copy-start | bytes 6881284
  80.5 49.1 %copy-start.29 = (f32[140,512]{1,0:T(8,128)S(1)}, f32[140,512]{1,0:T(8,128)}, u32[]{:S(2)}) copy-start(f32[140,512]{1,0:T(8,128)} %get-tuple-element.43) | copy-start | bytes 860164
  83.8 49.9 %copy-start.12 = (f32[140,512]{1,0:T(8,128)}, f32[140,512]{1,0:T(8,128)S(1)}, u32[]{:S(2)}) copy-start(f32[140,512]{1,0:T(8,128)S(1)} %get-tuple-element.18) | copy-start | bytes 860164
  83.8 59.7 %copy-start.17 = (f32[140,512]{1,0:T(8,128)}, f32[140,512]{1,0:T(8,128)S(1)}, u32[]{:S(2)}) copy-start(f32[140,512]{1,0:T(8,128)S(1)} %get-tuple-element.19) | copy-start | bytes 860164
  83.8 49.8 %collective-permute-start.5 = (f32[1,512]{1,0:T(1,128)S(1)}, f32[1,512]{1,0:T(1,128)S(1)}, u32[]{:S(2)}, u32[]{:S(2)}) collective-permute-start(f32[1,512]{1,0:T(1,128)S(1)} %slice.70), channel_id=1, source_target_pairs={{30,0},{0,2},{2,4},{4,6},{6,8},{8,10},{10,12},{12,14},{14,16},{16,... | collective-permute-start | bytes 6152 | tf_op jit(solution)/shard_map/ppermute | solution.py:18
  86.2 49.1 %collective-permute-start.2 = (f32[1,8,512]{2,1,0:T(8,128)S(1)}, f32[1,8,512]{2,1,0:T(8,128)S(1)}, u32[]{:S(2)}, u32[]{:S(2)}) collective-permute-start(f32[1,8,512]{2,1,0:T(8,128)S(1)} %slice.65), channel_id=1, source_target_pairs={{2,0},{4,2},{6,4},{8,6},{10,8},{12,10},{14,12},{16,14},{18,16},{20... | collective-permute-start | bytes 49160 | tf_op jit(solution)/shard_map/ppermute | solution.py:18
  127.1 6.3 %copy-start.32 = (f32[8,512]{1,0:T(8,128)S(1)}, f32[8,512]{1,0:T(8,128)}, u32[]{:S(2)}) copy-start(f32[8,512]{1,0:T(8,128)} %param.31) | copy-start | bytes 49156
  127.2 6.3 %copy-start.33 = (f32[8,512]{1,0:T(8,128)S(1)}, f32[8,512]{1,0:T(8,128)}, u32[]{:S(2)}) copy-start(f32[8,512]{1,0:T(8,128)} %param.22) | copy-start | bytes 49156
  136.1 7.4 %collective-permute-start.3 = (f32[1,8,512]{2,1,0:T(8,128)S(1)}, f32[1,8,512]{2,1,0:T(8,128)S(1)}, u32[]{:S(2)}, u32[]{:S(2)}) collective-permute-start(f32[1,8,512]{2,1,0:T(8,128)S(1)} %slice.66), channel_id=1, source_target_pairs={{30,0},{0,2},{2,4},{4,6},{6,8},{8,10},{10,12},{12,14},{14,16},{16,... | collective-permute-start | bytes 49160 | tf_op jit(solution)/shard_map/ppermute | solution.py:18
  137.4 6.1 %copy-start.11 = (f32[140,8,512]{2,1,0:T(8,128)S(1)}, f32[140,8,512]{2,1,0:T(8,128)}, u32[]{:S(2)}) copy-start(f32[140,8,512]{2,1,0:T(8,128)} %param.34) | copy-start | bytes 6881284
  191.7 43.9 %copy-start.4 = (f32[140,8,512]{2,1,0:T(8,128)S(1)}, f32[140,8,512]{2,1,0:T(8,128)}, u32[]{:S(2)}) copy-start(f32[140,8,512]{2,1,0:T(8,128)} %copy-done.2) | copy-start | bytes 6881284
  191.7 43.9 %copy-start.8 = (f32[140,8,512]{2,1,0:T(8,128)S(1)}, f32[140,8,512]{2,1,0:T(8,128)}, u32[]{:S(2)}) copy-start(f32[140,8,512]{2,1,0:T(8,128)} %get-tuple-element.22) | copy-start | bytes 6881284
  239.6 3.7 %collective-permute-start.7 = (f32[1,8,512]{2,1,0:T(8,128)S(1)}, f32[1,8,512]{2,1,0:T(8,128)S(1)}, u32[]{:S(2)}, u32[]{:S(2)}) collective-permute-start(f32[1,8,512]{2,1,0:T(8,128)S(1)} %slice.75), channel_id=1, source_target_pairs={{2,0},{4,2},{6,4},{8,6},{10,8},{12,10},{14,12},{16,14},{18,16},{20... | collective-permute-start | bytes 49160 | tf_op jit(solution)/shard_map/ppermute | solution.py:18
  242.0 3.6 %collective-permute-start.6 = (f32[1,512]{1,0:T(1,128)S(1)}, f32[1,512]{1,0:T(1,128)S(1)}, u32[]{:S(2)}, u32[]{:S(2)}) collective-permute-start(f32[1,512]{1,0:T(1,128)S(1)} %slice.73), channel_id=1, source_target_pairs={{2,0},{4,2},{6,4},{8,6},{10,8},{12,10},{14,12},{16,14},{18,16},{20... | collective-permute-start | bytes 6152 | tf_op jit(solution)/shard_map/ppermute | solution.py:18
  (21 other events, 45.8 us)
